TPU v7x, 256 devices: a whole 4x4x8 slice. The times are simulated.
256 devices in a mesh: frame: 8 (over z_hi, core), rank: 32 (over x, y, z_lo).
Axes of the slice: x: 4, y: 4, z: 8 (z_hi: 4, z_lo: 2; z = z_hi * 2 + z_lo), core: 2. Of those that a mesh axis runs over, the one named last changes fastest.
Arguments:
- layers: float32 [8, 32, 4, 32, 16384], P('frame', 'rank')
- depth_order: int32 [8, 32], P('frame'), may hold values from 0 to 31, as said below
- tile_slots: int32 [32], replicated, may hold values from 0 to 31, each once
Outputs:
- filtered: float32 [32, 8, 4, 16384], P('frame', None, None, 'rank')
- coverage: float32 [8], P('frame')
Inputs may be any that keep to these rules, and one draw needn't show every extreme that they name: `depth_order`: each row is a permutation of the ranks in which, for every bit b, the ranks that agree on all bits from b upward take consecutive depths. `tile_slots`: slot s belongs to frame group s // 4.
All inputs are finite; a program needn't handle non-finite values.
Results may differ from a plain program's by a relative error of at most 0.00002.
Values sent between devices are 32-bit elements; how exact they have to be, the bound alone decides.
A program may use at most 64 MiB of HBM per device.

v0:
```python
import jax
import jax.numpy as jnp
from jax import lax
from jax.sharding import PartitionSpec as P


def from_partner(value, axis, apart):
    mask = 2**apart
    pairs = [(source, source ^ mask) for source in range(lax.axis_size(axis))]
    return lax.ppermute(value, axis, pairs)


def sent_to_all(value, axis):
    count = lax.axis_size(axis)
    return lax.all_to_all(
        jnp.broadcast_to(value[None], (count, *value.shape)), axis, 0, 0, tiled=True
    )


def of_everyone(value, axis):
    everything = sent_to_all(value, axis)
    return jnp.sum(everything, axis=0)


def smooth_frames(block):
    before = jnp.concatenate([block[:, :, :1], block[:, :, :-1]], axis=2)
    after = jnp.concatenate([block[:, :, 1:], block[:, :, -1:]], axis=2)
    return 0.25 * before + 0.5 * block + 0.25 * after


def shards(layers, depth_order, tile_slots):
    mine = layers[0, 0]
    order = depth_order[0]
    ranks = lax.axis_size("rank")
    groups = lax.axis_size("frame")
    me_index = lax.axis_index("rank")
    channels, tile_count, pixels = mine.shape
    piece = pixels // ranks
    rank_ids = jnp.arange(ranks, dtype=jnp.int32)
    depth_of = jnp.sum(
        rank_ids[:, None] * (order[:, None] == rank_ids[None, :]).astype(jnp.int32), axis=0
    )
    levels = ranks.bit_length() - 1
    current = mine.reshape(channels, tile_count, ranks, piece)
    for level in range(levels):
        count = current.shape[2]
        halves = current.reshape(channels, tile_count, count // 2, 2, piece)
        upper = me_index >> level & 1 == 1
        keep = jnp.where(upper, halves[:, :, :, 1], halves[:, :, :, 0])
        give = jnp.where(upper, halves[:, :, :, 0], halves[:, :, :, 1])
        received = from_partner(give, "rank", level)
        partner = me_index ^ 1 << level
        nearer = depth_of[me_index] < depth_of[partner]
        front = jnp.where(nearer, keep, received)
        back = jnp.where(nearer, received, keep)
        current = front + (1.0 - front[3:4]) * back
    composite = current.reshape(channels, tile_count, piece)
    opacity = of_everyone(jnp.sum(composite[3]), "rank")
    coverage = (opacity / (tile_count * pixels)).reshape(1)
    picked = jnp.transpose(composite[:, tile_slots, :], (1, 0, 2))
    per_group = tile_count // groups
    picked = picked.reshape(groups, per_group, 1, channels, piece)
    filtered = smooth_frames(
        lax.all_to_all(picked, "frame", split_axis=0, concat_axis=2, tiled=True)
    )
    filtered = filtered.reshape(per_group, groups, channels, piece)
    return (filtered, coverage)


def solution(mesh):
    placed = (P("frame", "rank", None, None, None), P("frame", None), P())
    return jax.shard_map(
        shards,
        mesh=mesh,
        in_specs=placed,
        out_specs=(P("frame", None, None, "rank"), P("frame")),
        check_vma=False,
    )
```

profile of v0, /device:TPU:4, one launch (start us, length us, event | category | flops | bytes accessed | tf_op | source)
XLA Modules:
  0.0 285.0 jit_solution(11340218440994183050)
XLA Ops:
  0.6 11.8 %reshape_reshape_squeeze.3 = f32[4,32,16,2,512]{4,3,2,1,0:T(2,128)} reshape(f32[1,1,4,32,16384]{4,3,2,1,0:T(8,128)} %param.3) | data formatting | bytes 16777216 | tf_op jit(solution)/shard_map/reshape;reshape;squeeze | solution.py:47
  12.4 17.0 %fusion.13 = (f32[4,32,16,1,512]{4,3,2,1,0:T(1,128)}, f32[4,32,16,1,512]{4,3,2,1,0:T(1,128)S(1)}, f32[4,32,16,1,512]{4,3,2,1,0:T(1,128)}) fusion(f32[4,32,16,2,512]{4,3,2,1,0:T(2,128)} %reshape_reshape_squeeze.3, pred[]{:T(512)S(6)} %eq.38), kind=kLoop, calls=%fused_computation.54 | loop fusion | flops 1048576 | bytes 20971520 | tf_op jit(solution)/shard_map/slice | solution.py:49
  29.4 2.5 copy.177
  31.9 1.9 collective-permute-start
  33.8 0.1 select_reduce_fusion
  33.9 0.7 fusion.15
  35.8 88.8 %collective-permute-done = f32[4,32,16,512]{3,2,1,0:T(8,128)} collective-permute-done((f32[4,32,16,512]{3,2,1,0:T(8,128)}, f32[4,32,16,512]{3,2,1,0:T(8,128)}, u32[]{:S(2)}, u32[]{:S(2)}) %collective-permute-start) | collective-permute-done | bytes 4194336 | tf_op jit(solution)/shard_map/ppermute | solution.py:10
  124.7 5.2 %broadcast_select_fusion.1 = f32[4,32,16,512]{3,2,1,0:T(8,128)S(1)} fusion(f32[4,32,16,512]{3,2,1,0:T(8,128)} %collective-permute-done, pred[]{:T(512)} %bitcast.5, f32[4,32,16,1,512]{4,3,2,1,0:T(1,128)} %get-tuple-element.20, f32[4,32,16,1,512]{4,3,2,1,0:T(1,128)} %get-tuple-element.18, pred[]{:T(512)S(6)} %eq.38), kind=kLoop, calls=%fused_computation.10 | loop fusion | flops 2097152 | bytes 16777218 | tf_op jit(solution)/shard_map/jit(_where)/select_n | solution.py:54
  129.9 0.1 fusion.2
  130.1 0.5 copy-done.3
  130.6 3.9 %multiply_add_fusion = f32[4,32,16,512]{3,2,1,0:T(8,128)S(1)} fusion(f32[4,32,16,512]{3,2,1,0:T(8,128)} %collective-permute-done, f32[32,16,512]{2,1,0:T(8,128)S(1)} %fusion.2, pred[]{:T(512)} %bitcast.5, f32[4,32,16,1,512]{4,3,2,1,0:T(1,128)S(1)} %copy-done.3, f32[4,32,16,1,512]{4,3,2,1,0:T(1,128)S(1)} %copy-done.2, pred[]{:T(512)S(6)} %eq.38), kind=kLoop, calls=%fused_computation.5 | loop fusion | flops 5242880 | bytes 17825794 | tf_op jit(solution)/shard_map/add | solution.py:56
  134.5 2.4 copy.127
  137.0 1.9 copy-done
  138.9 1.8 select_bitcast_fusion
  140.7 1.6 collective-permute-start.1
  143.6 45.1 %collective-permute-done.1 = f32[4,32,8,512]{3,1,2,0:T(8,128)S(1)} collective-permute-done((f32[4,32,8,512]{3,1,2,0:T(8,128)}, f32[4,32,8,512]{3,1,2,0:T(8,128)S(1)}, u32[]{:S(2)}, u32[]{:S(2)}) %collective-permute-start.1) | collective-permute-done | bytes 2097184 | tf_op jit(solution)/shard_map/ppermute | solution.py:10
  188.7 3.8 %broadcast_select_fusion.2 = f32[4,32,8,512]{3,1,2,0:T(8,128)S(1)} fusion(f32[4,32,8,512]{3,1,2,0:T(8,128)S(1)} %collective-permute-done.1, pred[]{:T(512)} %bitcast.4, f32[4,32,8,2,512]{4,1,3,2,0:T(8,128)} %bitcast.134, pred[]{:T(512)S(6)} %eq.37), kind=kLoop, calls=%fused_computation.17 | loop fusion | flops 1048576 | bytes 8388610 | tf_op jit(solution)/shard_map/jit(_where)/select_n | solution.py:54
  192.5 0.4 copy-done.1
  192.9 2.4 multiply_add_fusion.1
  195.3 1.2 select_bitcast_fusion.1
  196.5 3.4 %collective-permute-start.2 = (f32[4,32,4,512]{3,1,2,0:T(8,128)}, f32[4,32,4,512]{3,1,2,0:T(8,128)S(1)}, u32[]{:S(2)}, u32[]{:S(2)}) collective-permute-start(f32[4,32,4,512]{3,1,2,0:T(8,128)} %select_bitcast_fusion.1), channel_id=1, source_target_pairs={{0,4},{1,5},{2,6},{3,7},{4,0},{5,1},{6,2},{7,3},{8,12},{9,13},{10,... | collective-permute-start | bytes 3145736 | tf_op jit(solution)/shard_map/ppermute | solution.py:10
  201.1 21.8 %collective-permute-done.2 = f32[4,32,4,512]{3,1,2,0:T(8,128)S(1)} collective-permute-done((f32[4,32,4,512]{3,1,2,0:T(8,128)}, f32[4,32,4,512]{3,1,2,0:T(8,128)S(1)}, u32[]{:S(2)}, u32[]{:S(2)}) %collective-permute-start.2) | collective-permute-done | bytes 1048608 | tf_op jit(solution)/shard_map/ppermute | solution.py:10
  222.9 0.3 broadcast_select_fusion.3
  223.3 0.4 multiply_add_fusion.2
  223.7 0.1 fusion.14
  223.8 0.6 select_bitcast_fusion.2
  224.4 0.5 collective-permute-start.3
  226.2 10.9 %collective-permute-done.3 = f32[4,32,2,512]{3,0,1,2:T(4,128)S(1)} collective-permute-done((f32[4,32,2,512]{3,0,1,2:T(4,128)S(1)}, f32[4,32,2,512]{3,0,1,2:T(4,128)S(1)}, u32[]{:S(2)}, u32[]{:S(2)}) %collective-permute-start.3) | collective-permute-done | bytes 524320 | tf_op jit(solution)/shard_map/ppermute | solution.py:10
  237.1 0.7 bitcast_select_fusion.3
  237.8 0.2 slice_subtract_fusion.3
  238.0 0.7 fusion.7
  238.7 0.1 select_bitcast_fusion.3
  238.8 0.1 collective-permute-start.4
  240.2 6.6 %collective-permute-done.4 = f32[4,32,1,512]{3,0,1,2:T(4,128)S(1)} collective-permute-done((f32[4,32,1,512]{3,0,1,2:T(4,128)S(1)}, f32[4,32,1,512]{3,0,1,2:T(4,128)S(1)}, u32[]{:S(2)}, u32[]{:S(2)}) %collective-permute-start.4) | collective-permute-done | bytes 262176 | tf_op jit(solution)/shard_map/ppermute | solution.py:10
  246.7 0.1 bitcast_select_fusion.5
  246.8 0.1 slice_subtract_fusion.4
  247.0 0.1 fusion.12
  247.1 0.7 slice_reduce_fusion
  247.8 1.2 broadcast_in_dim.5
  249.1 7.5 %all-to-all-start.1 = ((f32[32,1,1]{2,1,0:T(1,128)}), f32[32,1,1]{2,1,0:T(1,128)S(1)}, u32[]{:S(2)}, u32[]{:S(2)}) async-start(f32[32,1,1]{2,1,0:T(1,128)} %broadcast_in_dim.5), calls=%async_computation.1 | async-start | bytes 32768 | tf_op jit(solution)/shard_map/all_to_all | solution.py:15
  256.6 1.4 gather_fusion
  258.0 4.6 %all-to-all-done.1 = f32[32,1,1]{2,1,0:T(1,128)S(1)} async-done(((f32[32,1,1]{2,1,0:T(1,128)}), f32[32,1,1]{2,1,0:T(1,128)S(1)}, u32[]{:S(2)}, u32[]{:S(2)}) %all-to-all-start.1) | async-done | bytes 160 | tf_op jit(solution)/shard_map/all_to_all | solution.py:15
  262.7 8.1 %all-to-all-start = ((f32[8,4,1,4,512]{4,3,1,2,0:T(4,128)}), f32[8,4,1,4,512]{4,3,1,2,0:T(4,128)S(1)}, u32[]{:S(2)}, u32[]{:S(2)}) async-start(f32[8,4,1,4,512]{4,3,1,2,0:T(4,128)} %bitcast.30), calls=%async_computation | async-start | bytes 524288 | tf_op jit(solution)/shard_map/all_to_all | solution.py:64
  270.7 0.6 reduce_sum.29
  272.0 10.9 %all-to-all-done = f32[8,4,1,4,512]{4,3,1,2,0:T(4,128)S(1)} async-done(((f32[8,4,1,4,512]{4,3,1,2,0:T(4,128)}), f32[8,4,1,4,512]{4,3,1,2,0:T(4,128)S(1)}, u32[]{:S(2)}, u32[]{:S(2)}) %all-to-all-start) | async-done | bytes 262176 | tf_op jit(solution)/shard_map/all_to_all | solution.py:64
  282.9 0.1 slice_bitcast_fusion
  283.0 0.2 fusion.10
  283.1 0.7 copy.140
  (18 shorter events, 0.1 us)
Async XLA Ops:
  29.4 4.4 %copy-start.5 = (s32[1,32]{1,0:T(1,128)S(1)}, s32[1,32]{1,0:T(1,128)}, u32[]{:S(2)}) copy-start(s32[1,32]{1,0:T(1,128)} %param.4) | copy-start | bytes 388
  31.9 92.8 %collective-permute-start = (f32[4,32,16,512]{3,2,1,0:T(8,128)}, f32[4,32,16,512]{3,2,1,0:T(8,128)}, u32[]{:S(2)}, u32[]{:S(2)}) collective-permute-start(f32[4,32,16,512]{3,2,1,0:T(8,128)} %bitcast.130), channel_id=1, source_target_pairs={{0,1},{1,0},{2,3},{3,2},{4,5},{5,4},{6,7},{7,6},{8,9},{9,8},{10,11... | collective-permute-start | bytes 12582920 | tf_op jit(solution)/shard_map/ppermute | solution.py:10
  124.7 5.4 %copy-start.2 = (f32[4,32,16,1,512]{4,3,2,1,0:T(1,128)S(1)}, f32[4,32,16,1,512]{4,3,2,1,0:T(1,128)}, u32[]{:S(2)}) copy-start(f32[4,32,16,1,512]{4,3,2,1,0:T(1,128)} %get-tuple-element.18) | copy-start | bytes 12582916
  124.7 5.9 %copy-start.3 = (f32[4,32,16,1,512]{4,3,2,1,0:T(1,128)S(1)}, f32[4,32,16,1,512]{4,3,2,1,0:T(1,128)}, u32[]{:S(2)}) copy-start(f32[4,32,16,1,512]{4,3,2,1,0:T(1,128)} %get-tuple-element.20) | copy-start | bytes 12582916
  136.9 2.0 copy-start
  140.7 47.9 %collective-permute-start.1 = (f32[4,32,8,512]{3,1,2,0:T(8,128)}, f32[4,32,8,512]{3,1,2,0:T(8,128)S(1)}, u32[]{:S(2)}, u32[]{:S(2)}) collective-permute-start(f32[4,32,8,512]{3,1,2,0:T(8,128)} %select_bitcast_fusion), channel_id=1, source_target_pairs={{0,2},{1,3},{2,0},{3,1},{4,6},{5,7},{6,4},{7,5},{8,10},{9,11},{10,... | collective-permute-start | bytes 6291464 | tf_op jit(solution)/shard_map/ppermute | solution.py:10
  188.6 3.8 %copy-start.4 = (f32[4,32,8,512]{3,1,2,0:T(8,128)}, f32[4,32,8,512]{3,1,2,0:T(8,128)S(1)}, u32[]{:S(2)}) copy-start(f32[4,32,8,512]{3,1,2,0:T(8,128)S(1)} %collective-permute-done.1) | copy-start | bytes 6291460
  188.6 4.2 %copy-start.1 = (f32[4,32,16,512]{3,1,2,0:T(8,128)S(1)}, f32[4,32,16,512]{3,1,2,0:T(8,128)}, u32[]{:S(2)}) copy-start(f32[4,32,16,512]{3,1,2,0:T(8,128)} %copy-done) | copy-start | bytes 12582916
  196.5 26.4 %collective-permute-start.2 = (f32[4,32,4,512]{3,1,2,0:T(8,128)}, f32[4,32,4,512]{3,1,2,0:T(8,128)S(1)}, u32[]{:S(2)}, u32[]{:S(2)}) collective-permute-start(f32[4,32,4,512]{3,1,2,0:T(8,128)} %select_bitcast_fusion.1), channel_id=1, source_target_pairs={{0,4},{1,5},{2,6},{3,7},{4,0},{5,1},{6,2},{7,3},{8,12},{9,13},{10,... | collective-permute-start | bytes 3145736 | tf_op jit(solution)/shard_map/ppermute | solution.py:10
  223.7 16.5 %copy-start.6 = (s32[32]{0:T(128)S(1)}, s32[32]{0:T(128)}, u32[]{:S(2)}) copy-start(s32[32]{0:T(128)} %param.5) | copy-start | bytes 388
  224.4 12.7 %collective-permute-start.3 = (f32[4,32,2,512]{3,0,1,2:T(4,128)S(1)}, f32[4,32,2,512]{3,0,1,2:T(4,128)S(1)}, u32[]{:S(2)}, u32[]{:S(2)}) collective-permute-start(f32[4,32,2,512]{3,0,1,2:T(4,128)S(1)} %select_bitcast_fusion.2), channel_id=1, source_target_pairs={{0,8},{1,9},{2,10},{3,11},{4,12},{5,13},{6,14},{7,15},{8,0},{9,1},... | collective-permute-start | bytes 1572872 | tf_op jit(solution)/shard_map/ppermute | solution.py:10
  238.8 8.0 %collective-permute-start.4 = (f32[4,32,1,512]{3,0,1,2:T(4,128)S(1)}, f32[4,32,1,512]{3,0,1,2:T(4,128)S(1)}, u32[]{:S(2)}, u32[]{:S(2)}) collective-permute-start(f32[4,32,1,512]{3,0,1,2:T(4,128)S(1)} %select_bitcast_fusion.3), channel_id=1, source_target_pairs={{0,16},{1,17},{2,18},{3,19},{4,20},{5,21},{6,22},{7,23},{8,24},{9,... | collective-permute-start | bytes 786440 | tf_op jit(solution)/shard_map/ppermute | solution.py:10
  249.1 13.6 %all-to-all-start.1 = ((f32[32,1,1]{2,1,0:T(1,128)}), f32[32,1,1]{2,1,0:T(1,128)S(1)}, u32[]{:S(2)}, u32[]{:S(2)}) async-start(f32[32,1,1]{2,1,0:T(1,128)} %broadcast_in_dim.5), calls=%async_computation.1 | async-start | bytes 32768 | tf_op jit(solution)/shard_map/all_to_all | solution.py:15
  262.7 20.2 %all-to-all-start = ((f32[8,4,1,4,512]{4,3,1,2,0:T(4,128)}), f32[8,4,1,4,512]{4,3,1,2,0:T(4,128)S(1)}, u32[]{:S(2)}, u32[]{:S(2)}) async-start(f32[8,4,1,4,512]{4,3,1,2,0:T(4,128)} %bitcast.30), calls=%async_computation | async-start | bytes 524288 | tf_op jit(solution)/shard_map/all_to_all | solution.py:64
where the time goes:
time: 287 us; the launch traced here: 285 us
  waiting for transfers between devices  189 us (66%)
  other arithmetic  40.6 us (14%)
  local copies, waits for them, and re-layouts  23.7 us (8%)
  starting transfers between devices  23.1 us (8%)
  between operations  8.9 us (3%)
    ppermute x5, waiting for transfers between devices, from_partner(): return lax.ppermute(value, axis, pairs)  173 us
    slice x1, other arithmetic, shards(): keep = jnp.where(upper, halves[:, :, :, 1], halves[:, :, :, 0])  17 us
    another operation x1, local copies, waits for them, and re-layouts, shards(): halves = current.reshape(channels, tile_count, count // 2, 2, piece)  11.8 us
    all_to_all x1, waiting for transfers between devices, shards(): lax.all_to_all(picked, 'frame', split_axis=0, concat_axis=2, tiled=True)  10.9 us
    select_n x5, other arithmetic, shards(): front = jnp.where(nearer, keep, received)  10.2 us
    all_to_all x1, starting transfers between devices, shards(): lax.all_to_all(picked, 'frame', split_axis=0, concat_axis=2, tiled=True)  8.06 us
    all_to_all x1, starting transfers between devices, sent_to_all(): lax.all_to_all(jnp.broadcast_to(value[None], (count, *value.shape)), axis...  7.54 us
    ppermute x5, starting transfers between devices, from_partner(): return lax.ppermute(value, axis, pairs)  7.49 us
  transfers between devices with their start and end apart: 7, of which 7 were waited for; matrix products, arithmetic and copies ran while one was open for 1% of the time, Pallas kernels for 0%

commit v1 on v0

v1 whole, which is shorter than its diff:
```python
import functools

import jax
import jax.numpy as jnp
from jax import lax
from jax.experimental import pallas as pl
from jax.experimental.pallas import tpu as pltpu
from jax.sharding import PartitionSpec as P

MESH = pl.DeviceIdType.MESH
LANES = 128
ROWS = 8
AHEAD = 2

CHUNKS = (
    ("alpha", 2, 0), ("alpha", 2, 1), ("swap", 0, 0),
    ("alpha", 2, 2), ("alpha", 2, 3), ("swap", 0, 2),
    ("alpha", 3, 0), ("alpha", 3, 1), ("swap", 1, 0),
    ("alpha", 3, 2), ("alpha", 3, 3), ("swap", 1, 2),
)


def blend(a, b, b_near):
    weight_a = 1.0 - b_near * b[:, 3:4]
    weight_b = 1.0 - (1.0 - b_near) * a[:, 3:4]
    return weight_a * a + weight_b * b


def blend4(values, flags):
    low = blend(values[0], values[1], flags[0])
    high = blend(values[2], values[3], flags[1])
    return blend(low, high, flags[2])


def kernel(
    layers, order, slots, out, cov,
    keep, half, alpha, ysend, ybuf, xsend, xbuf, vsend, vrecv, comp, chosen, picked, fbuf, csend, cbuf,
    keep_sem, zs, zr, ys, yr, xs, xr, vs, vr, fs, fr, cs, cr,
):
    rank = lax.axis_index("rank")
    frame = lax.axis_index("frame")
    x, y, z = lax.div(rank, 8), lax.rem(lax.div(rank, 2), 4), lax.rem(rank, 2)
    frames = fbuf.shape[1]
    pixels = layers.shape[1] * layers.shape[2]

    def at(px, py, pz):
        return {"rank": px * 8 + py * 2 + pz}

    partner = at(x, y, 1 - z)

    barrier = pltpu.get_barrier_semaphore()

    def greet(device):
        pl.semaphore_signal(barrier, inc=1, device_id=device, device_id_type=MESH)

    greet(partner)
    for d in range(1, 4):
        greet(at(x, lax.rem(y + d, 4), z))
        greet(at(lax.rem(x + d, 4), y, z))
    for d in range(1, frames):
        greet({"frame": lax.rem(frame + d, frames)})

    def tiles(group):
        return pl.ds(group * ROWS, ROWS)

    def rows_of(group):
        return slice(group * ROWS, (group + 1) * ROWS)

    def lanes(px, py, pz, tile):
        start = ((px * 8 + py * 2 + pz) * 4 + tile) * LANES
        return pl.ds(pl.multiple_of(start, LANES), LANES)

    kinds = [kind for kind, _, _ in CHUNKS]
    number = [kinds[:i].count(kind) for i, kind in enumerate(kinds)]

    def load_own(c):
        kind, tile, group = CHUNKS[c]

        def body(q, carry):
            py, px = lax.div(q, 4), lax.rem(q, 4)
            for u in range(2):
                if kind == "swap":
                    source = layers.at[:, tiles(group + u), lanes(px, py, z, tile)]
                else:
                    source = layers.at[:, tiles(group), lanes(px, py, u, tile)]
                pltpu.make_async_copy(source, keep.at[c, q, u], keep_sem.at[c]).start()
            return carry

        lax.fori_loop(0, 16, body, 0)

    def send_z(c):
        kind, tile, group = CHUNKS[c]
        n = number[c]

        def body(q, carry):
            py, px = lax.div(q, 4), lax.rem(q, 4)
            for u in range(2):
                if kind == "swap":
                    source = layers.at[:, tiles(group + u), lanes(px, py, 1 - z, tile)]
                    target = half.at[n, q, u]
                else:
                    source = layers.at[3, tiles(group), lanes(px, py, u, tile)]
                    target = alpha.at[n, q, u]
                remote(source, target, zs.at[c], zr.at[c], partner).start()
            return carry

        lax.fori_loop(0, 16, body, 0)

    def remote(src, dst, send_sem, recv_sem, device):
        return pltpu.make_async_remote_copy(
            src_ref=src, dst_ref=dst, send_sem=send_sem, recv_sem=recv_sem, device_id=device, device_id_type=MESH
        )

    def z_copy(c):
        box = half.at[number[c]] if kinds[c] == "swap" else alpha.at[number[c]]
        return remote(box, box, zs.at[c], zr.at[c], partner)

    def y_copy(c, d):
        return remote(ysend.at[c, d - 1], ybuf.at[c, d], ys.at[c, d - 1], yr.at[c, d - 1], at(x, lax.rem(y + d, 4), z))

    def x_copy(c, d):
        return remote(xsend.at[c, d - 1], xbuf.at[c, d], xs.at[c, d - 1], xr.at[c, d - 1], at(lax.rem(x + d, 4), y, z))

    def v_copy(c):
        n = number[c]
        return remote(vsend.at[n], vrecv.at[n], vs.at[n], vr.at[n], partner)

    def f_copy(tile, d):
        return remote(
            picked.at[tile, d], fbuf.at[tile, d], fs.at[tile, d - 1], fr.at[tile, d - 1],
            {"frame": lax.rem(frame + d, frames)},
        )

    def c_copy(phase, d):
        device = (at(lax.rem(x + d, 4), y, z), at(x, lax.rem(y + d, 4), z), partner)[phase]
        return remote(
            csend.at[phase], cbuf.at[phase, d - 1], cs.at[phase, d - 1], cr.at[phase, d - 1], device
        )

    for c in range(AHEAD):
        load_own(c)

    own_pair = (at(x, y, 0)["rank"], at(x, y, 1)["rank"])
    wanted = own_pair + tuple(at(x, k, 0)["rank"] for k in range(4)) + tuple(at(k, 0, 0)["rank"] for k in range(4))

    def find(k, found):
        here = order[k]
        return tuple(jnp.where(here == who, k, depth) for who, depth in zip(wanted, found))

    depth = lax.fori_loop(0, 32, find, (jnp.int32(0),) * len(wanted))

    def nearer(first, second):
        return jnp.where(depth[second] < depth[first], jnp.float32(1), jnp.float32(0))

    second_near = nearer(0, 1)
    partner_near = jnp.where(z == 0, second_near, 1.0 - second_near)
    y_flags = (nearer(2, 3), nearer(4, 5), nearer(2, 4))
    x_flags = (nearer(6, 7), nearer(8, 9), nearer(6, 8))

    row = lax.broadcasted_iota(jnp.int32, chosen.shape, 0)
    column = lax.broadcasted_iota(jnp.int32, chosen.shape, 1)
    wanted_tile = jnp.zeros(chosen.shape, jnp.int32)
    for d in range(frames):
        for j in range(4):
            wanted_tile = jnp.where(row // 4 == d * 4 + j, slots[lax.rem(frame + d, frames) * 4 + j], wanted_tile)
    hit = column == row % 4 * comp.shape[2] + wanted_tile
    chosen[...] = jnp.where(hit, jnp.float32(1), jnp.float32(0))

    pl.semaphore_wait(barrier, 1 + 6 + frames - 1)
    for c in range(AHEAD):
        send_z(c)

    def pair(c):
        kind = kinds[c]
        n = number[c]
        pltpu.make_async_copy(keep.at[c], keep.at[c], keep_sem.at[c]).wait()
        z_copy(c).wait_recv()

        def value(q):
            own = keep[c, q]
            if kind == "swap":
                return blend(own, half[n, q], partner_near)
            other = alpha[n, q]
            weight = 1.0 - partner_near * other
            opacity = weight * own[:, 3] + (1.0 - (1.0 - partner_near) * own[:, 3]) * other
            return jnp.concatenate([weight[:, None] * own[:, :3], opacity[:, None]], axis=1)

        for d in (2, 1, 3, 0):
            py = lax.rem(y + d, 4)

            def body(px, carry, d=d, py=py):
                result = value(py * 4 + px)
                if d == 0:
                    ybuf[c, 0, px] = result
                else:
                    ysend[c, d - 1, px] = result
                return carry

            lax.fori_loop(0, 4, body, 0)
            if d:
                y_copy(c, d).start()

    def over_y(c):
        for d in range(1, 4):
            y_copy(c, d).wait_recv()
        for d in (2, 1, 3, 0):
            px = lax.rem(x + d, 4)
            result = blend4([ybuf[c, lax.rem(y - k + 4, 4), px] for k in range(4)], y_flags)
            if d == 0:
                xbuf[c, 0] = result
            else:
                xsend[c, d - 1] = result
                x_copy(c, d).start()

    def over_x(c):
        kind, tile, group = CHUNKS[c]
        for d in range(1, 4):
            x_copy(c, d).wait_recv()
        result = blend4([xbuf[c, lax.rem(x - k + 4, 4)] for k in range(4)], x_flags)
        low, high = result[0], result[1]
        if kind == "swap":
            comp[tile, :, rows_of(group)] = low
            comp[tile, :, rows_of(group + 1)] = high
            csend[0] += low[3] + high[3]
        else:
            n = number[c]
            mine = jnp.where(z == 0, low, high)
            vsend[n] = jnp.where(z == 0, high, low)[:3]
            v_copy(c).start()
            comp[tile, :, rows_of(group)] = mine
            csend[0] += mine[3]

    def add_z(c):
        kind, tile, group = CHUNKS[c]
        v_copy(c).wait_recv()
        comp[tile, :3, rows_of(group)] += vrecv[number[c]]

    def send_frames(tile):
        picked[tile] = jnp.dot(
            chosen[...],
            comp[tile].reshape(4 * comp.shape[2], LANES),
            preferred_element_type=jnp.float32,
            precision=lax.Precision.HIGHEST,
        ).reshape(picked.shape[1:])
        for d in range(1, frames):
            f_copy(tile, d).start()
        fbuf[tile, 0] = picked[tile, 0]

    def smooth(tile):
        for d in range(1, frames):
            f_copy(tile, d).wait_recv()
        values = [fbuf[tile, lax.rem(frame - k + frames, frames)] for k in range(frames)]
        for k in range(frames):
            before, after = values[max(k - 1, 0)], values[min(k + 1, frames - 1)]
            result = 0.25 * before + 0.5 * values[k] + 0.25 * after
            for j in range(4):
                out[j, k, :, tile * LANES : (tile + 1) * LANES] = result[j * 4 : (j + 1) * 4]

    csend[0] = jnp.zeros((ROWS, LANES), jnp.float32)
    count = len(CHUNKS)
    left = [sum(tile == t for _, tile, _ in CHUNKS) for t in range(4)]
    sent = []

    def finished(c):
        tile = CHUNKS[c][1]
        left[tile] -= 1
        if left[tile] == 0:
            send_frames(tile)
            sent.append(tile)

    for step in range(count + 3):
        if step < count:
            if step + AHEAD < count:
                load_own(step + AHEAD)
                send_z(step + AHEAD)
            pair(step)
        if 0 <= step - 1 < count:
            over_y(step - 1)
        if 0 <= step - 2 < count:
            over_x(step - 2)
            if kinds[step - 2] == "swap":
                finished(step - 2)
        if 0 <= step - 3 < count and kinds[step - 3] == "alpha":
            add_z(step - 3)
            finished(step - 3)

    for phase, peers in enumerate((3, 3, 1)):
        for d in range(1, peers + 1):
            c_copy(phase, d).start()
        total = csend[phase]
        for d in range(1, peers + 1):
            c_copy(phase, d).wait_recv()
            total = total + cbuf[phase, d - 1]
        csend[phase + 1] = total
    cov[0] = jnp.sum(csend[3]) / pixels

    for t in sent:
        smooth(t)

    for c in range(count):
        z_copy(c).wait_send()
        for d in range(1, 4):
            y_copy(c, d).wait_send()
            x_copy(c, d).wait_send()
        if kinds[c] == "alpha":
            v_copy(c).wait_send()
    for t in sent:
        for d in range(1, frames):
            f_copy(t, d).wait_send()
    for phase, peers in enumerate((3, 3, 1)):
        for d in range(1, peers + 1):
            c_copy(phase, d).wait_send()


def shards(layers, depth_order, tile_slots):
    mine = layers[0, 0]
    frames = lax.axis_size("frame")
    count = len(CHUNKS)
    swaps = sum(kind == "swap" for kind, _, _ in CHUNKS)
    alphas = count - swaps
    block = (2, 4, ROWS, LANES)
    vmem = functools.partial(pltpu.VMEM, dtype=jnp.float32)
    dma = pltpu.SemaphoreType.DMA
    filtered, coverage = pl.pallas_call(
        kernel,
        out_shape=(
            jax.ShapeDtypeStruct((4, frames, 4, 4 * LANES), jnp.float32),
            jax.ShapeDtypeStruct((1,), jnp.float32),
        ),
        in_specs=[
            pl.BlockSpec(memory_space=pltpu.HBM),
            pl.BlockSpec(memory_space=pltpu.SMEM),
            pl.BlockSpec(memory_space=pltpu.SMEM),
        ],
        out_specs=(pl.BlockSpec(memory_space=pltpu.VMEM), pl.BlockSpec(memory_space=pltpu.SMEM)),
        scratch_shapes=[
            vmem((count, 16, *block)),
            vmem((swaps, 16, *block)),
            vmem((alphas, 16, 2, ROWS, LANES)),
            vmem((count, 3, 4, *block)),
            vmem((count, 4, 4, *block)),
            vmem((count, 3, *block)),
            vmem((count, 4, *block)),
            vmem((alphas, 3, ROWS, LANES)),
            vmem((alphas, 3, ROWS, LANES)),
            vmem((4, 4, 32, LANES)),
            vmem((16 * frames, 4 * 32)),
            vmem((4, frames, 16, LANES)),
            vmem((4, frames, 16, LANES)),
            vmem((4, ROWS, LANES)),
            vmem((3, 3, ROWS, LANES)),
            dma((count,)),
            dma((count,)),
            dma((count,)),
            dma((count, 3)),
            dma((count, 3)),
            dma((count, 3)),
            dma((count, 3)),
            dma((alphas,)),
            dma((alphas,)),
            dma((4, frames - 1)),
            dma((4, frames - 1)),
            dma((3, 3)),
            dma((3, 3)),
        ],
        compiler_params=pltpu.CompilerParams(
            collective_id=0, has_side_effects=True, vmem_limit_bytes=56 * 1024 * 1024
        ),
        name="composite",
    )(mine, depth_order[0], tile_slots)
    return (filtered, coverage)


def solution(mesh):
    placed = (P("frame", "rank", None, None, None), P("frame", None), P())
    return jax.shard_map(
        shards,
        mesh=mesh,
        in_specs=placed,
        out_specs=(P("frame", None, None, "rank"), P("frame")),
        check_vma=False,
    )
```

time: 287 us -> 112 us (0.39)
  waiting for transfers between devices: 189 us -> 0 us
  Pallas kernels: 0 us -> 108 us
  other arithmetic: 40.6 us -> 0 us
  starting transfers between devices: 23.1 us -> 0 us
  local copies, waits for them, and re-layouts: 23.7 us -> 1.67 us
  between operations: 8.9 us -> 2.4 us
    ppermute x5 -> x0, waiting for transfers between devices: 173 us -> none  [from_partner(): return lax.ppermute(value, axis, pairs)]
    pallas_call x0 -> x1, Pallas kernels: none -> 108 us  [shards(): pl.pallas_call(kernel, out_shape=(jax.ShapeDtypeStruct((4, frames, 4, 4 *...]
    slice x1 -> x0, other arithmetic: 17 us -> none  [shards(): keep = jnp.where(upper, halves[:, :, :, 1], halves[:, :, :, 0])]
    all_to_all x2 -> x0, starting transfers between devices: 15.6 us -> none  [the longest x1 8.06 us: shards(): lax.all_to_all(picked, 'frame', split_axis=0, concat_axis=2, tiled=True)]
    all_to_all x2 -> x0, waiting for transfers between devices: 15.5 us -> none  [the longest x1 10.9 us: shards(): lax.all_to_all(picked, 'frame', split_axis=0, concat_axis=2, tiled=True)]
    select_n x10 -> x0, other arithmetic: 13.9 us -> none  [the longest x5 10.2 us: shards(): front = jnp.where(nearer, keep, received)]
    another operation x1 -> x0, local copies, waits for them, and re-layouts: 11.8 us -> none  [shards(): halves = current.reshape(channels, tile_count, count // 2, 2, piece)]
    ppermute x5 -> x0, starting transfers between devices: 7.49 us -> none  [from_partner(): return lax.ppermute(value, axis, pairs)]
  transfers between devices with their start and end apart: 7 -> 0, of which waited for: 7 -> 0; matrix products, arithmetic and copies ran while one was open for 1% -> 0% of each run, Pallas kernels for 0% -> 0%
where the time goes in v1:
time: 112 us
  Pallas kernels  108 us (96%)
  between operations  2.4 us (2%)
  local copies, waits for them, and re-layouts  1.67 us (1%)
    pallas_call x1, Pallas kernels, shards(): pl.pallas_call(kernel, out_shape=(jax.ShapeDtypeStruct((4, frames, 4, 4 *...  108 us

profile of v1, /device:TPU:4, one launch (start us, length us, event | category | flops | bytes accessed | tf_op | source)
XLA Modules:
  0.0 112.2 jit_solution(18382520963053696232)
XLA Ops:
  0.6 108.1 %composite.1 = (f32[4,8,4,512]{3,2,1,0:T(4,128)}, f32[1]{0:T(128)}) custom-call(f32[4,32,16384]{2,1,0:T(8,128)} %bitcast.2, s32[32]{0:T(128)} %bitcast.3, s32[32]{0:T(128)} %slots.1), custom_call_target="tpu_custom_call" | custom-call | tf_op jit(solution)/shard_map/composite/pallas_call | solution.py:324
  108.7 1.7 %copy.7 = f32[4,8,4,512]{3,2,1,0:T(4,128)} copy(f32[4,8,4,512]{3,2,1,0:T(4,128)} %get-tuple-element.4) | data formatting | bytes 524288

commit v2 on v1

--- a/solution.py
+++ b/solution.py
@@ -10,14 +10,19 @@
 MESH = pl.DeviceIdType.MESH
 LANES = 128
 ROWS = 8
-AHEAD = 2
 
 CHUNKS = (
-    ("alpha", 2, 0), ("alpha", 2, 1), ("swap", 0, 0),
-    ("alpha", 2, 2), ("alpha", 2, 3), ("swap", 0, 2),
-    ("alpha", 3, 0), ("alpha", 3, 1), ("swap", 1, 0),
-    ("alpha", 3, 2), ("alpha", 3, 3), ("swap", 1, 2),
+    *(("alpha", tile, group) for tile in (2, 3) for group in range(4)),
+    ("alpha", 0, 0),
+    *(("swap", 0, group) for group in range(1, 4)),
+    *(("swap", 1, group) for group in range(4)),
 )
+LAG_X, LAG_V = 3, 5
+SUM_PEERS = (3, 3, 1)
+UNITS = {"alpha": 2, "swap": 1}
+SEND_Z = {"alpha": 2.9, "swap": 5.6}
+SEND_Y = {"alpha": 5.9, "swap": 2.95}
+LEAD = 0.0
 
 
 def blend(a, b, b_near):
@@ -34,13 +39,18 @@
 
 def kernel(
     layers, order, slots, out, cov,
-    keep, half, alpha, ysend, ybuf, xsend, xbuf, vsend, vrecv, comp, chosen, picked, fbuf, csend, cbuf,
+    keep_a, keep_s, half, alpha, ysend_a, ysend_s, ybuf_a, ybuf_s, xsend_a, xsend_s, xbuf_a, xbuf_s, vsend, vrecv, comp, chosen, picked, fbuf, csend, cbuf,
     keep_sem, zs, zr, ys, yr, xs, xr, vs, vr, fs, fr, cs, cr,
 ):
     rank = lax.axis_index("rank")
     frame = lax.axis_index("frame")
     x, y, z = lax.div(rank, 8), lax.rem(lax.div(rank, 2), 4), lax.rem(rank, 2)
     frames = fbuf.shape[1]
+    keep = {"alpha": keep_a, "swap": keep_s}
+    ysend = {"alpha": ysend_a, "swap": ysend_s}
+    ybuf = {"alpha": ybuf_a, "swap": ybuf_s}
+    xsend = {"alpha": xsend_a, "swap": xsend_s}
+    xbuf = {"alpha": xbuf_a, "swap": xbuf_s}
     pixels = layers.shape[1] * layers.shape[2]
 
     def at(px, py, pz):
@@ -53,12 +63,12 @@
     def greet(device):
         pl.semaphore_signal(barrier, inc=1, device_id=device, device_id_type=MESH)
 
-    greet(partner)
+    for d in range(1, frames):
+        greet({"frame": lax.rem(frame + d, frames)})
     for d in range(1, 4):
         greet(at(x, lax.rem(y + d, 4), z))
         greet(at(lax.rem(x + d, 4), y, z))
-    for d in range(1, frames):
-        greet({"frame": lax.rem(frame + d, frames)})
+    greet(partner)
 
     def tiles(group):
         return pl.ds(group * ROWS, ROWS)
@@ -78,12 +88,12 @@
 
         def body(q, carry):
             py, px = lax.div(q, 4), lax.rem(q, 4)
-            for u in range(2):
+            for u in range(UNITS[kind]):
                 if kind == "swap":
-                    source = layers.at[:, tiles(group + u), lanes(px, py, z, tile)]
+                    source = layers.at[:, tiles(group), lanes(px, py, z, tile)]
                 else:
                     source = layers.at[:, tiles(group), lanes(px, py, u, tile)]
-                pltpu.make_async_copy(source, keep.at[c, q, u], keep_sem.at[c]).start()
+                pltpu.make_async_copy(source, keep[kind].at[number[c], q, u], keep_sem.at[c]).start()
             return carry
 
         lax.fori_loop(0, 16, body, 0)
@@ -94,9 +104,9 @@
 
         def body(q, carry):
             py, px = lax.div(q, 4), lax.rem(q, 4)
-            for u in range(2):
+            for u in range(UNITS[kind]):
                 if kind == "swap":
-                    source = layers.at[:, tiles(group + u), lanes(px, py, 1 - z, tile)]
+                    source = layers.at[:, tiles(group), lanes(px, py, 1 - z, tile)]
                     target = half.at[n, q, u]
                 else:
                     source = layers.at[3, tiles(group), lanes(px, py, u, tile)]
@@ -116,10 +126,12 @@
         return remote(box, box, zs.at[c], zr.at[c], partner)
 
     def y_copy(c, d):
-        return remote(ysend.at[c, d - 1], ybuf.at[c, d], ys.at[c, d - 1], yr.at[c, d - 1], at(x, lax.rem(y + d, 4), z))
+        kind, n = kinds[c], number[c]
+        return remote(ysend[kind].at[n, d - 1], ybuf[kind].at[n, d], ys.at[c, d - 1], yr.at[c, d - 1], at(x, lax.rem(y + d, 4), z))
 
     def x_copy(c, d):
-        return remote(xsend.at[c, d - 1], xbuf.at[c, d], xs.at[c, d - 1], xr.at[c, d - 1], at(lax.rem(x + d, 4), y, z))
+        kind, n = kinds[c], number[c]
+        return remote(xsend[kind].at[n, d - 1], xbuf[kind].at[n, d], xs.at[c, d - 1], xr.at[c, d - 1], at(lax.rem(x + d, 4), y, z))
 
     def v_copy(c):
         n = number[c]
@@ -137,8 +149,8 @@
             csend.at[phase], cbuf.at[phase, d - 1], cs.at[phase, d - 1], cr.at[phase, d - 1], device
         )
 
-    for c in range(AHEAD):
-        load_own(c)
+    load_own(0)
+    load_own(1)
 
     own_pair = (at(x, y, 0)["rank"], at(x, y, 1)["rank"])
     wanted = own_pair + tuple(at(x, k, 0)["rank"] for k in range(4)) + tuple(at(k, 0, 0)["rank"] for k in range(4))
@@ -167,17 +179,18 @@
     chosen[...] = jnp.where(hit, jnp.float32(1), jnp.float32(0))
 
     pl.semaphore_wait(barrier, 1 + 6 + frames - 1)
-    for c in range(AHEAD):
-        send_z(c)
+    send_z(0)
+    send_z(1)
 
     def pair(c):
         kind = kinds[c]
         n = number[c]
-        pltpu.make_async_copy(keep.at[c], keep.at[c], keep_sem.at[c]).wait()
+        own_all = keep[kind].at[n]
+        pltpu.make_async_copy(own_all, own_all, keep_sem.at[c]).wait()
         z_copy(c).wait_recv()
 
         def value(q):
-            own = keep[c, q]
+            own = keep[kind][n, q]
             if kind == "swap":
                 return blend(own, half[n, q], partner_near)
             other = alpha[n, q]
@@ -191,9 +204,9 @@
             def body(px, carry, d=d, py=py):
                 result = value(py * 4 + px)
                 if d == 0:
-                    ybuf[c, 0, px] = result
+                    ybuf[kind][n, 0, px] = result
                 else:
-                    ysend[c, d - 1, px] = result
+                    ysend[kind][n, d - 1, px] = result
                 return carry
 
             lax.fori_loop(0, 4, body, 0)
@@ -201,28 +214,28 @@
                 y_copy(c, d).start()
 
     def over_y(c):
+        kind, n = kinds[c], number[c]
         for d in range(1, 4):
             y_copy(c, d).wait_recv()
         for d in (2, 1, 3, 0):
             px = lax.rem(x + d, 4)
-            result = blend4([ybuf[c, lax.rem(y - k + 4, 4), px] for k in range(4)], y_flags)
+            result = blend4([ybuf[kind][n, lax.rem(y - k + 4, 4), px] for k in range(4)], y_flags)
             if d == 0:
-                xbuf[c, 0] = result
+                xbuf[kind][n, 0] = result
             else:
-                xsend[c, d - 1] = result
+                xsend[kind][n, d - 1] = result
                 x_copy(c, d).start()
 
     def over_x(c):
         kind, tile, group = CHUNKS[c]
         for d in range(1, 4):
             x_copy(c, d).wait_recv()
-        result = blend4([xbuf[c, lax.rem(x - k + 4, 4)] for k in range(4)], x_flags)
-        low, high = result[0], result[1]
+        result = blend4([xbuf[kind][number[c], lax.rem(x - k + 4, 4)] for k in range(4)], x_flags)
         if kind == "swap":
-            comp[tile, :, rows_of(group)] = low
-            comp[tile, :, rows_of(group + 1)] = high
-            csend[0] += low[3] + high[3]
+            comp[tile, :, rows_of(group)] = result[0]
+            csend[0] += result[0, 3]
         else:
+            low, high = result[0], result[1]
             n = number[c]
             mine = jnp.where(z == 0, low, high)
             vsend[n] = jnp.where(z == 0, high, low)[:3]
@@ -268,34 +281,51 @@
             send_frames(tile)
             sent.append(tile)
 
-    for step in range(count + 3):
-        if step < count:
-            if step + AHEAD < count:
-                load_own(step + AHEAD)
-                send_z(step + AHEAD)
-            pair(step)
-        if 0 <= step - 1 < count:
-            over_y(step - 1)
-        if 0 <= step - 2 < count:
-            over_x(step - 2)
-            if kinds[step - 2] == "swap":
-                finished(step - 2)
-        if 0 <= step - 3 < count and kinds[step - 3] == "alpha":
-            add_z(step - 3)
-            finished(step - 3)
-
-    for phase, peers in enumerate((3, 3, 1)):
-        for d in range(1, peers + 1):
+    def start_sum(phase):
+        for d in range(1, SUM_PEERS[phase] + 1):
             c_copy(phase, d).start()
+
+    def end_sum(phase):
         total = csend[phase]
-        for d in range(1, peers + 1):
+        for d in range(1, SUM_PEERS[phase] + 1):
             c_copy(phase, d).wait_recv()
             total = total + cbuf[phase, d - 1]
         csend[phase + 1] = total
-    cov[0] = jnp.sum(csend[3]) / pixels
-
-    for t in sent:
+
+    issued = 2
+    z_time = SEND_Z[kinds[0]] + SEND_Z[kinds[1]]
+    y_time = 0.0
+    for step in range(count + LAG_V):
+        if step < count:
+            pair(step)
+            y_time += SEND_Y[kinds[step]]
+            while issued < count and (issued <= step + 1 or z_time < y_time + LEAD):
+                load_own(issued)
+                send_z(issued)
+                z_time += SEND_Z[kinds[issued]]
+                issued += 1
+        if 0 <= step - 1 < count:
+            over_y(step - 1)
+        done = step - LAG_X
+        if 0 <= done < count:
+            over_x(done)
+            if done == count - 1:
+                start_sum(0)
+            if kinds[done] == "swap":
+                finished(done)
+        done = step - LAG_V
+        if 0 <= done < count and kinds[done] == "alpha":
+            add_z(done)
+            finished(done)
+
+    for t in sent[:-1]:
         smooth(t)
+    for phase in range(len(SUM_PEERS)):
+        if phase:
+            start_sum(phase)
+        end_sum(phase)
+    cov[0] = jnp.sum(csend[len(SUM_PEERS)]) / pixels
+    smooth(sent[-1])
 
     for c in range(count):
         z_copy(c).wait_send()
@@ -307,7 +337,7 @@
     for t in sent:
         for d in range(1, frames):
             f_copy(t, d).wait_send()
-    for phase, peers in enumerate((3, 3, 1)):
+    for phase, peers in enumerate(SUM_PEERS):
         for d in range(1, peers + 1):
             c_copy(phase, d).wait_send()
 
@@ -318,7 +348,7 @@
     count = len(CHUNKS)
     swaps = sum(kind == "swap" for kind, _, _ in CHUNKS)
     alphas = count - swaps
-    block = (2, 4, ROWS, LANES)
+    block = {"alpha": (2, 4, ROWS, LANES), "swap": (1, 4, ROWS, LANES)}
     vmem = functools.partial(pltpu.VMEM, dtype=jnp.float32)
     dma = pltpu.SemaphoreType.DMA
     filtered, coverage = pl.pallas_call(
@@ -334,13 +364,18 @@
         ],
         out_specs=(pl.BlockSpec(memory_space=pltpu.VMEM), pl.BlockSpec(memory_space=pltpu.SMEM)),
         scratch_shapes=[
-            vmem((count, 16, *block)),
-            vmem((swaps, 16, *block)),
+            vmem((alphas, 16, *block["alpha"])),
+            vmem((swaps, 16, *block["swap"])),
+            vmem((swaps, 16, *block["swap"])),
             vmem((alphas, 16, 2, ROWS, LANES)),
-            vmem((count, 3, 4, *block)),
-            vmem((count, 4, 4, *block)),
-            vmem((count, 3, *block)),
-            vmem((count, 4, *block)),
+            vmem((alphas, 3, 4, *block["alpha"])),
+            vmem((swaps, 3, 4, *block["swap"])),
+            vmem((alphas, 4, 4, *block["alpha"])),
+            vmem((swaps, 4, 4, *block["swap"])),
+            vmem((alphas, 3, *block["alpha"])),
+            vmem((swaps, 3, *block["swap"])),
+            vmem((alphas, 4, *block["alpha"])),
+            vmem((swaps, 4, *block["swap"])),
             vmem((alphas, 3, ROWS, LANES)),
             vmem((alphas, 3, ROWS, LANES)),
             vmem((4, 4, 32, LANES)),

time: 112 us -> 109 us (0.973)
  Pallas kernels: 108 us -> 105 us
    pallas_call x1, Pallas kernels: 108 us -> 105 us  [shards(): pl.pallas_call(kernel, out_shape=(jax.ShapeDtypeStruct((4, frames, 4, 4 *...]
where the time goes in v2:
time: 109 us
  Pallas kernels  105 us (96%)
  between operations  2.4 us (2%)
  local copies, waits for them, and re-layouts  1.67 us (2%)
    pallas_call x1, Pallas kernels, shards(): pl.pallas_call(kernel, out_shape=(jax.ShapeDtypeStruct((4, frames, 4, 4 *...  105 us

profile of v2, /device:TPU:4, one launch (start us, length us, event | category | flops | bytes accessed | tf_op | source)
XLA Modules:
  0.0 108.7 jit_solution(3906894768412514748)
XLA Ops:
  0.6 104.6 %composite.1 = (f32[4,8,4,512]{3,2,1,0:T(4,128)}, f32[1]{0:T(128)}) custom-call(f32[4,32,16384]{2,1,0:T(8,128)} %bitcast.2, s32[32]{0:T(128)} %bitcast.3, s32[32]{0:T(128)} %slots.1), custom_call_target="tpu_custom_call" | custom-call | tf_op jit(solution)/shard_map/composite/pallas_call | solution.py:354
  105.2 1.7 %copy.7 = f32[4,8,4,512]{3,2,1,0:T(4,128)} copy(f32[4,8,4,512]{3,2,1,0:T(4,128)} %get-tuple-element.4) | data formatting | bytes 524288

commit v3 on v2

--- a/solution.py
+++ b/solution.py
@@ -17,7 +17,7 @@
     *(("swap", 0, group) for group in range(1, 4)),
     *(("swap", 1, group) for group in range(4)),
 )
-LAG_X, LAG_V = 3, 5
+LAG_X, LAG_V = 4, 6
 SUM_PEERS = (3, 3, 1)
 UNITS = {"alpha": 2, "swap": 1}
 SEND_Z = {"alpha": 2.9, "swap": 5.6}
@@ -149,8 +149,8 @@
             csend.at[phase], cbuf.at[phase, d - 1], cs.at[phase, d - 1], cr.at[phase, d - 1], device
         )
 
-    load_own(0)
-    load_own(1)
+    for c in range(16):
+        load_own(c)
 
     own_pair = (at(x, y, 0)["rank"], at(x, y, 1)["rank"])
     wanted = own_pair + tuple(at(x, k, 0)["rank"] for k in range(4)) + tuple(at(k, 0, 0)["rank"] for k in range(4))
@@ -300,7 +300,6 @@
             pair(step)
             y_time += SEND_Y[kinds[step]]
             while issued < count and (issued <= step + 1 or z_time < y_time + LEAD):
-                load_own(issued)
                 send_z(issued)
                 z_time += SEND_Z[kinds[issued]]
                 issued += 1

time: 109 us -> 108 us (level)
  no operation moved by 1% of the time
where the time goes in v3:
time: 108 us
  Pallas kernels  104 us (96%)
  between operations  2.4 us (2%)
  local copies, waits for them, and re-layouts  1.67 us (2%)
    pallas_call x1, Pallas kernels, shards(): pl.pallas_call(kernel, out_shape=(jax.ShapeDtypeStruct((4, frames, 4, 4 *...  104 us

profile of v3, /device:TPU:4, one launch (start us, length us, event | category | flops | bytes accessed | tf_op | source)
XLA Modules:
  0.0 108.3 jit_solution(15433533128999690065)
XLA Ops:
  0.6 104.2 %composite.1 = (f32[4,8,4,512]{3,2,1,0:T(4,128)}, f32[1]{0:T(128)}) custom-call(f32[4,32,16384]{2,1,0:T(8,128)} %bitcast.2, s32[32]{0:T(128)} %bitcast.3, s32[32]{0:T(128)} %slots.1), custom_call_target="tpu_custom_call" | custom-call | tf_op jit(solution)/shard_map/composite/pallas_call | solution.py:353
  104.9 1.7 %copy.7 = f32[4,8,4,512]{3,2,1,0:T(4,128)} copy(f32[4,8,4,512]{3,2,1,0:T(4,128)} %get-tuple-element.4) | data formatting | bytes 524288
